TPU v7x, 32 devices: a whole 2x2x4 slice. The times are simulated.
32 devices in a mesh: dp: 4 (over y, x), expert: 8 (over z, core).
Axes of the slice: x: 2, y: 2, z: 4, core: 2. Of those that a mesh axis runs over, the one named last changes fastest.
Arguments:
- images: bfloat16 [32, 197, 768], P(('dp', 'expert')), may hold values from -6 to 6
- ln1_gain: bfloat16 [768], P(('dp', 'expert')), may hold values from 0.25 to 1.75
- ln1_bias: bfloat16 [768], P(('dp', 'expert')), may hold values from -3 to 3
- qkv_weight: bfloat16 [768, 2304], P(('dp', 'expert')), may hold values from -0.21875 to 0.21875
- q_bias: bfloat16 [768], P(('dp', 'expert')), may hold values from -3 to 3
- v_bias: bfloat16 [768], P(('dp', 'expert')), may hold values from -3 to 3
- out_weight: bfloat16 [768, 768], P(('dp', 'expert')), may hold values from -0.875 to 0.875
- out_bias: bfloat16 [768], P(('dp', 'expert')), may hold values from -3 to 3
- ln2_gain: bfloat16 [768], P(('dp', 'expert')), may hold values from 0.25 to 1.75
- ln2_bias: bfloat16 [768], P(('dp', 'expert')), may hold values from -3 to 3
- in_weight: bfloat16 [8, 768, 3072], P('expert'), may hold values from -0.21875 to 0.21875
- in_bias: bfloat16 [8, 3072], P('expert'), may hold values from -3 to 3
- down_weight: bfloat16 [8, 3072, 768], P('expert'), may hold values from -0.109375 to 0.109375
- down_bias: bfloat16 [8, 768], P('expert'), may hold values from -3 to 3
- routes: int32 [32, 197, 2], P(('dp', 'expert')), may hold values from 0 to 7, all different within a row; in each aligned block of 197 rows (0 to 196, 197 to 393, ..., all dimensions but the last counted through in order) at most 50 rows name the same one
- gate_weights: float32 [32, 197, 2], P(('dp', 'expert')), may hold values from 0.1 to 1
- grad_out: bfloat16 [32, 197, 768], P(('dp', 'expert')), may hold values from -6 to 6
Outputs:
- block_output: bfloat16 [32, 197, 768], P(('dp', 'expert'))
- image_grad: float32 [32, 197, 768], P(('dp', 'expert'))
- ln1_gain_grad: float32 [768], P(('dp', 'expert'))
- ln1_bias_grad: float32 [768], P(('dp', 'expert'))
- qkv_weight_grad: float32 [768, 2304], P(('dp', 'expert'))
- q_bias_grad: float32 [768], P(('dp', 'expert'))
- v_bias_grad: float32 [768], P(('dp', 'expert'))
- out_weight_grad: float32 [768, 768], P(('dp', 'expert'))
- out_bias_grad: float32 [768], P(('dp', 'expert'))
- ln2_gain_grad: float32 [768], P(('dp', 'expert'))
- ln2_bias_grad: float32 [768], P(('dp', 'expert'))
- in_weight_grad: float32 [8, 768, 3072], P('expert', None, 'dp')
- in_bias_grad: float32 [8, 3072], P('expert', 'dp')
- down_weight_grad: float32 [8, 3072, 768], P('expert', 'dp')
- down_bias_grad: float32 [8, 768], P('expert', 'dp')
Inputs may be any that keep to these rules, and one draw needn't show every extreme that they name: `routes`: in each aligned block of 197 rows (the tokens of one device) no expert is named more than 50 times, a bound that some block reaches; the two experts of a token differ.
All inputs are finite; a program needn't handle non-finite values.
Results may differ from a plain program's by a relative error of at most 0.012.
Values may be sent and summed in bfloat16 or wider, within the bound.
No kernel may reach another device: no remote copies, remote signals or barrier semaphores. Data moves between devices by JAX's collectives and lax.ppermute only.
A program may use at most 192 MiB of HBM per device.

v0:
```python
import jax
import jax.numpy as jnp
from jax import lax
from jax.sharding import PartitionSpec as P

D = 768
HEADS = 12
HEAD_DIM = 64
SEQ = 197
EPSILON = 1e-06


def to_half(values):
    return lax.optimization_barrier(values.astype(jnp.bfloat16))


def layer_norm(values, gain, shift):
    average = jnp.mean(values, axis=-1, keepdims=True)
    centred = values - average
    inverse = lax.rsqrt(jnp.mean(centred * centred, axis=-1, keepdims=True) + EPSILON)
    normal = centred * inverse
    return (normal * gain.astype(jnp.float32) + shift.astype(jnp.float32), normal, inverse)


def norm_back(upstream, normal, inverse, gain):
    weighted = upstream * gain.astype(jnp.float32)
    first_mean = jnp.mean(weighted, axis=-1, keepdims=True)
    second_mean = jnp.mean(weighted * normal, axis=-1, keepdims=True)
    return inverse * (weighted - first_mean - normal * second_mean)


def slot_positions(flat_routes, expert_count, capacity):
    onehot = (flat_routes[:, None] == jnp.arange(expert_count, dtype=jnp.int32)[None, :]).astype(
        jnp.int32
    )
    earlier = jnp.cumsum(onehot, axis=0) - onehot
    return flat_routes * capacity + jnp.sum(earlier * onehot, axis=1)


def split_heads(projected, image_count):
    parts = projected.reshape(image_count, SEQ, 3, HEADS, HEAD_DIM)
    return (parts[:, :, 0], parts[:, :, 1], parts[:, :, 2])


def head_scores(queries, key_heads):
    return jnp.einsum(
        "bqhd,bkhd->bhqk", queries, key_heads, preferred_element_type=jnp.float32
    ) * HEAD_DIM ** (-0.5)


def per_device(
    images,
    ln1_gain,
    ln1_bias,
    qkv_weight,
    q_bias,
    v_bias,
    out_weight,
    out_bias,
    ln2_gain,
    ln2_bias,
    in_weight,
    in_bias,
    down_weight,
    down_bias,
    routes,
    gate_weights,
    grad_out,
):
    gathered = (
        lax.all_gather(ln1_gain, ("dp", "expert"), axis=0, tiled=True),
        lax.all_gather(ln1_bias, ("dp", "expert"), axis=0, tiled=True),
        lax.all_gather(qkv_weight, ("dp", "expert"), axis=0, tiled=True),
        lax.all_gather(q_bias, ("dp", "expert"), axis=0, tiled=True),
        lax.all_gather(v_bias, ("dp", "expert"), axis=0, tiled=True),
        lax.all_gather(out_weight, ("dp", "expert"), axis=0, tiled=True),
        lax.all_gather(out_bias, ("dp", "expert"), axis=0, tiled=True),
        lax.all_gather(ln2_gain, ("dp", "expert"), axis=0, tiled=True),
        lax.all_gather(ln2_bias, ("dp", "expert"), axis=0, tiled=True),
    )
    (
        full_gain_one,
        full_bias_one,
        full_qkv,
        full_q_bias,
        full_v_bias,
        full_out,
        full_out_bias,
        full_gain_two,
        full_bias_two,
    ) = gathered
    image_count = images.shape[0]
    token_count = image_count * SEQ
    inputs = images.reshape(token_count, D).astype(jnp.float32)
    normed_one, normal_one, inverse_one = layer_norm(inputs, full_gain_one, full_bias_one)
    normed_one = to_half(normed_one)
    bias_row = jnp.concatenate(
        [
            full_q_bias.astype(jnp.float32),
            jnp.zeros((D,), jnp.float32),
            full_v_bias.astype(jnp.float32),
        ]
    )
    projected = to_half(
        jnp.dot(normed_one, full_qkv, preferred_element_type=jnp.float32) + bias_row
    )
    queries, key_heads, value_heads = split_heads(projected, image_count)
    scores = head_scores(queries, key_heads)
    log_total = jnp.log(jnp.sum(jnp.exp(scores), axis=-1, keepdims=True))
    attention = to_half(jnp.exp(scores - log_total))
    context = jnp.einsum(
        "bhqk,bkhd->bqhd", attention, value_heads, preferred_element_type=jnp.float32
    )
    context = context.astype(jnp.bfloat16).reshape(token_count, D)
    residual = (
        inputs
        + jnp.dot(context, full_out, preferred_element_type=jnp.float32)
        + full_out_bias.astype(jnp.float32)
    )
    normed_two, normal_two, inverse_two = layer_norm(residual, full_gain_two, full_bias_two)
    normed_two = to_half(normed_two)
    expert_count = lax.axis_size("expert")
    capacity = max(2, (2 * token_count + expert_count - 1) // expert_count)
    slot_total = expert_count * capacity
    positions = slot_positions(routes.reshape(2 * token_count), expert_count, capacity)
    mixing = gate_weights.reshape(2 * token_count, 1)
    outgoing = (
        jnp.zeros((slot_total, D), jnp.bfloat16)
        .at[positions]
        .set(jnp.repeat(normed_two, 2, axis=0))
    )
    received = lax.all_to_all(
        outgoing.reshape(expert_count, capacity, D),
        "expert",
        split_axis=0,
        concat_axis=0,
        tiled=True,
    ).reshape(slot_total, D)
    weight_in = in_weight[0]
    weight_down = down_weight[0]
    hidden_pre = jnp.dot(received, weight_in, preferred_element_type=jnp.float32) + in_bias[
        0
    ].astype(jnp.float32)
    activated = to_half(jax.nn.gelu(hidden_pre))
    expert_result = to_half(
        jnp.dot(activated, weight_down, preferred_element_type=jnp.float32)
        + down_bias[0].astype(jnp.float32)
    )
    returned = lax.all_to_all(
        expert_result.reshape(expert_count, capacity, D),
        "expert",
        split_axis=0,
        concat_axis=0,
        tiled=True,
    ).reshape(slot_total, D)
    picked = returned[positions].astype(jnp.float32)
    mixture = jnp.sum((picked * mixing).reshape(token_count, 2, D), axis=1)
    block_output = (residual + mixture).astype(jnp.bfloat16).reshape(images.shape)
    upstream = grad_out.reshape(token_count, D).astype(jnp.float32)
    routed_grads = to_half(jnp.repeat(upstream, 2, axis=0) * mixing)
    grad_buffer = jnp.zeros((slot_total, D), jnp.bfloat16).at[positions].set(routed_grads)
    routed_in = lax.all_to_all(
        grad_buffer.reshape(expert_count, capacity, D),
        "expert",
        split_axis=0,
        concat_axis=0,
        tiled=True,
    ).reshape(slot_total, D)
    grad_hidden = jnp.dot(routed_in, weight_down.T, preferred_element_type=jnp.float32)
    grad_pre = to_half(jax.vjp(jax.nn.gelu, hidden_pre)[1](grad_hidden)[0])
    grad_rows = to_half(jnp.dot(grad_pre, weight_in.T, preferred_element_type=jnp.float32))
    grad_returned = lax.all_to_all(
        grad_rows.reshape(expert_count, capacity, D),
        "expert",
        split_axis=0,
        concat_axis=0,
        tiled=True,
    ).reshape(slot_total, D)
    local_in = jnp.dot(received.T, grad_pre, preferred_element_type=jnp.float32)
    local_down = jnp.dot(activated.T, routed_in, preferred_element_type=jnp.float32)
    local_bias_in = jnp.sum(grad_pre.astype(jnp.float32), axis=0)
    local_bias_down = jnp.sum(routed_in.astype(jnp.float32), axis=0)
    grad_weight_in, grad_weight_down, grad_bias_in, grad_bias_down = (
        lax.psum_scatter(
            local_in.astype(jnp.bfloat16), "dp", scatter_dimension=1, tiled=True
        ).astype(jnp.float32),
        lax.psum_scatter(
            local_down.astype(jnp.bfloat16), "dp", scatter_dimension=0, tiled=True
        ).astype(jnp.float32),
        lax.psum_scatter(
            local_bias_in.astype(jnp.bfloat16), "dp", scatter_dimension=0, tiled=True
        ).astype(jnp.float32),
        lax.psum_scatter(
            local_bias_down.astype(jnp.bfloat16), "dp", scatter_dimension=0, tiled=True
        ).astype(jnp.float32),
    )
    grad_normed_two = jnp.sum(
        grad_returned[positions].astype(jnp.float32).reshape(token_count, 2, D), axis=1
    )
    ln2_gain_grad = jnp.sum(grad_normed_two * normal_two, axis=0)
    ln2_bias_grad = jnp.sum(grad_normed_two, axis=0)
    grad_residual = upstream + norm_back(grad_normed_two, normal_two, inverse_two, full_gain_two)
    out_bias_grad = jnp.sum(grad_residual, axis=0)
    branch_grad = to_half(grad_residual)
    out_weight_grad = jnp.dot(context.T, branch_grad, preferred_element_type=jnp.float32)
    grad_context = to_half(jnp.dot(branch_grad, full_out.T, preferred_element_type=jnp.float32))
    probable = jnp.exp(head_scores(queries, key_heads) - log_total)
    incoming = grad_context.reshape(image_count, SEQ, HEADS, HEAD_DIM)
    grad_values = jnp.einsum(
        "bhqk,bqhd->bkhd", attention, incoming, preferred_element_type=jnp.float32
    )
    grad_probs = jnp.einsum(
        "bqhd,bkhd->bhqk", incoming, value_heads, preferred_element_type=jnp.float32
    )
    centre = jnp.sum(probable * grad_probs, axis=-1, keepdims=True)
    grad_scores = to_half(probable * (grad_probs - centre) * HEAD_DIM ** (-0.5))
    grad_queries = jnp.einsum(
        "bhqk,bkhd->bqhd", grad_scores, key_heads, preferred_element_type=jnp.float32
    )
    grad_keys = jnp.einsum(
        "bhqk,bqhd->bkhd", grad_scores, queries, preferred_element_type=jnp.float32
    )
    grad_projected = jnp.stack([grad_queries, grad_keys, grad_values], axis=2).reshape(
        token_count, 3 * D
    )
    q_bias_grad = jnp.sum(grad_projected[:, :D], axis=0)
    v_bias_grad = jnp.sum(grad_projected[:, 2 * D :], axis=0)
    projected_grad = to_half(grad_projected)
    qkv_weight_grad = jnp.dot(normed_one.T, projected_grad, preferred_element_type=jnp.float32)
    grad_normed_one = jnp.dot(projected_grad, full_qkv.T, preferred_element_type=jnp.float32)
    ln1_gain_grad = jnp.sum(grad_normed_one * normal_one, axis=0)
    ln1_bias_grad = jnp.sum(grad_normed_one, axis=0)
    image_grad = (
        grad_residual + norm_back(grad_normed_one, normal_one, inverse_one, full_gain_one)
    ).reshape(images.shape)
    summed = (
        lax.psum_scatter(ln1_gain_grad, ("dp", "expert"), scatter_dimension=0, tiled=True),
        lax.psum_scatter(ln1_bias_grad, ("dp", "expert"), scatter_dimension=0, tiled=True),
        lax.psum_scatter(qkv_weight_grad, ("dp", "expert"), scatter_dimension=0, tiled=True),
        lax.psum_scatter(q_bias_grad, ("dp", "expert"), scatter_dimension=0, tiled=True),
        lax.psum_scatter(v_bias_grad, ("dp", "expert"), scatter_dimension=0, tiled=True),
        lax.psum_scatter(out_weight_grad, ("dp", "expert"), scatter_dimension=0, tiled=True),
        lax.psum_scatter(out_bias_grad, ("dp", "expert"), scatter_dimension=0, tiled=True),
        lax.psum_scatter(ln2_gain_grad, ("dp", "expert"), scatter_dimension=0, tiled=True),
        lax.psum_scatter(ln2_bias_grad, ("dp", "expert"), scatter_dimension=0, tiled=True),
    )
    (
        gain_one_share,
        bias_one_share,
        qkv_share,
        q_bias_share,
        v_bias_share,
        out_share,
        out_bias_share,
        gain_two_share,
        bias_two_share,
    ) = summed
    return (
        block_output,
        image_grad,
        gain_one_share,
        bias_one_share,
        qkv_share,
        q_bias_share,
        v_bias_share,
        out_share,
        out_bias_share,
        gain_two_share,
        bias_two_share,
        grad_weight_in[None],
        grad_bias_in[None],
        grad_weight_down[None],
        grad_bias_down[None],
    )


def solution(mesh):
    in_specs = (
        P(("dp", "expert"), None, None),
        P(("dp", "expert")),
        P(("dp", "expert")),
        P(("dp", "expert"), None),
        P(("dp", "expert")),
        P(("dp", "expert")),
        P(("dp", "expert"), None),
        P(("dp", "expert")),
        P(("dp", "expert")),
        P(("dp", "expert")),
        P("expert", None, None),
        P("expert", None),
        P("expert", None, None),
        P("expert", None),
        P(("dp", "expert"), None, None),
        P(("dp", "expert"), None, None),
        P(("dp", "expert"), None, None),
    )
    out_specs = (
        P(("dp", "expert"), None, None),
        P(("dp", "expert"), None, None),
        P(("dp", "expert")),
        P(("dp", "expert")),
        P(("dp", "expert"), None),
        P(("dp", "expert")),
        P(("dp", "expert")),
        P(("dp", "expert"), None),
        P(("dp", "expert")),
        P(("dp", "expert")),
        P(("dp", "expert")),
        P("expert", None, "dp"),
        P("expert", "dp"),
        P("expert", "dp", None),
        P("expert", "dp"),
    )
    return jax.shard_map(
        per_device, mesh=mesh, in_specs=in_specs, out_specs=out_specs, check_vma=False
    )
```

profile of v0, /device:TPU:0, one launch (start us, length us, event | category | flops | bytes accessed | tf_op | source)
XLA Modules:
  0.0 538.8 jit_solution(14895257947561775607)
XLA Ops:
  14.2 2.3 scatter_custom_fusion.1
  17.6 6.4 %all-to-all-start.2 = ((bf16[8,50,768]{2,1,0:T(8,128)(2,1)}), bf16[8,50,768]{2,1,0:T(8,128)(2,1)}, u32[]{:S(2)}, u32[]{:S(2)}) async-start(bf16[8,50,768]{2,1,0:T(8,128)(2,1)} %reshape.261), calls=%async_computation.2 | async-start | bytes 1376256 | tf_op jit(solution)/shard_map/all_to_all | solution.py:162
  26.3 42.0 %all-reduce.18 = (bf16[768]{0:T(1024)(128)(2,1)S(1)}, bf16[768]{0:T(1024)(128)(2,1)S(1)}, bf16[768]{0:T(1024)(128)(2,1)S(1)}, bf16[768]{0:T(1024)(128)(2,1)S(1)}...) all-reduce(bf16[768]{0:T(1024)(128)(2,1)S(1)} %dynamic-update-slice, ...), channel_id=1, replica_groups=mesh['dp'=4,'expert'=8] {'dp','expert'}, use_global_device_ids=true, to_apply=%add.2 | all-reduce | flops 5376 | bytes 21504
  69.1 6.3 %all-gather.3.cloned.1.call-done = bf16[768,2304]{1,0:T(8,128)(2,1)} async-done(((bf16[24,2304]{1,0:T(8,128)(2,1)}), bf16[768,2304]{1,0:T(8,128)(2,1)}) %all-gather.3.cloned.1.call-update) | async-done | bytes 3538960 | tf_op jit(solution)/shard_map/all_gather | solution.py:73
  75.4 2.9 fusion.17
  80.5 2.1 fusion.20
  83.7 1.3 convolution_convert_fusion.2
  85.1 46.3 %all-gather.5.cloned.1.call-done = bf16[768,768]{1,0:T(8,128)(2,1)} async-done(((bf16[24,768]{1,0:T(8,128)(2,1)}), bf16[768,768]{1,0:T(8,128)(2,1)}) %all-gather.5.cloned.1.call-update) | async-done | bytes 1179664 | tf_op jit(solution)/shard_map/all_gather | solution.py:76
  131.4 1.8 fusion.75
  136.0 2.7 reshape.299
  138.6 2.9 scatter_custom_fusion
  142.5 3.5 all-to-all-start
  146.7 2.1 reshape.262
  148.8 16.1 %all-to-all-done = bf16[8,50,768]{2,1,0:T(8,128)(2,1)S(1)} async-done(((bf16[8,50,768]{2,1,0:T(8,128)(2,1)}), bf16[8,50,768]{2,1,0:T(8,128)(2,1)S(1)}, u32[]{:S(2)}, u32[]{:S(2)}) %all-to-all-start) | async-done | bytes 614432 | tf_op jit(solution)/shard_map/all_to_all | solution.py:132
  165.8 7.2 %multiply_convert_fusion = (bf16[400,3072]{1,0:T(8,128)(2,1)}, f32[400,3072]{1,0:T(8,128)S(1)}) fusion(f32[3072]{0:T(1024)S(1)} %bitcast.175, bf16[400,768]{1,0:T(8,128)(2,1)} %reshape.256, bf16[1,768,3072]{2,1,0:T(8,128)(2,1)} %param.27), kind=kOutput, calls=%fused_computation.17 | convolution fusion | flops 1899724800 | bytes 12718080 | tf_op jit(solution)/shard_map/dot_general | solution.py:141
  173.1 7.5 %fusion.8 = bf16[400,3072]{1,0:T(8,128)(2,1)S(1)} fusion(f32[400,3072]{1,0:T(8,128)S(1)} %get-tuple-element.91, bf16[400,768]{1,0:T(8,128)(2,1)S(1)} %copy-done.19, bf16[1,3072,768]{2,1,0:T(8,128)(2,1)} %param.29, f32[3072]{0:T(1024)S(1)} %bitcast.176), kind=kOutput, calls=%fused_computation.16 | convolution fusion | flops 1913241600 | bytes 12718080 | tf_op jit(solution)/shard_map/dot_general | solution.py:169
  180.6 1.5 copy-done.15
  182.1 4.3 convolution_convert_fusion.1
  186.5 6.5 %convolution_convert_fusion = bf16[3072,768]{1,0:T(8,128)(2,1)} fusion(bf16[400,3072]{1,0:T(8,128)(2,1)} %get-tuple-element.90, bf16[400,768]{1,0:T(8,128)(2,1)S(1)} %copy-done.19), kind=kOutput, calls=%fused_computation.8 | convolution fusion | flops 1889796096 | bytes 7790592 | tf_op jit(solution)/shard_map/dot_general | solution.py:180
  193.0 5.2 fusion.37
  199.2 3.7 all-to-all-start.3
  203.0 6.3 %fusion.34 = bf16[400,768]{1,0:T(8,128)(2,1)} fusion(bf16[400,3072]{1,0:T(8,128)(2,1)} %get-tuple-element.90, bf16[1,3072,768]{2,1,0:T(8,128)(2,1)} %param.29, f32[768]{0:T(1024)S(1)} %convert_reduce_fusion.2), kind=kOutput, calls=%fused_computation.39 | convolution fusion | flops 1888051200 | bytes 7793664 | tf_op jit(solution)/shard_map/dot_general | solution.py:146
  209.3 2.1 reshape.257
  211.4 10.3 %all-to-all-done.3 = bf16[8,50,768]{2,1,0:T(8,128)(2,1)S(1)} async-done(((bf16[8,50,768]{2,1,0:T(8,128)(2,1)}), bf16[8,50,768]{2,1,0:T(8,128)(2,1)S(1)}, u32[]{:S(2)}, u32[]{:S(2)}) %all-to-all-start.3) | async-done | bytes 614432 | tf_op jit(solution)/shard_map/all_to_all | solution.py:172
  221.7 4.2 all-to-all-start.1
  226.8 1.3 pad_clamp_fusion
  229.3 2.8 gather_fusion.1
  232.1 2.8 reshape.274
  234.9 3.6 reduce_sum.214
  238.5 6.3 %all-to-all-done.1 = bf16[8,50,768]{2,1,0:T(8,128)(2,1)} async-done(((bf16[8,50,768]{2,1,0:T(8,128)(2,1)}), bf16[8,50,768]{2,1,0:T(8,128)(2,1)}, u32[]{:S(2)}, u32[]{:S(2)}) %all-to-all-start.1) | async-done | bytes 614432 | tf_op jit(solution)/shard_map/all_to_all | solution.py:149
  246.1 2.7 gather_fusion
  248.7 2.8 reshape.272
  251.6 2.3 multiply_reduce_fusion.2
  253.9 2.8 multiply_reduce_fusion.1
  258.6 1.9 fusion.77
  260.8 1.9 convolution_convert_fusion.3
  262.9 3.1 fusion.28
  266.0 2.0 convolution_bitcast_fusion
  270.4 4.1 fusion.76
  278.3 2.1 reduce_sum.227
  280.4 10.0 %all-reduce.19 = (bf16[3072]{0:T(1024)(128)(2,1)S(1)}, bf16[768]{0:T(1024)(128)(2,1)S(1)}) all-reduce(bf16[3072]{0:T(1024)(128)(2,1)S(1)} %reduce_sum.227, bf16[768]{0:T(1024)(128)(2,1)S(1)} %reduce_sum.228), channel_id=12, replica_groups=mesh['dp'=4,'expert'=8] {'dp'}, use_global_device_ids=true, to_apply=%region_35.36.clone | all-reduce | flops 3840 | bytes 15360
  291.7 4.0 fusion.60
  296.0 1.4 copy.64
  297.9 37.3 %all-reduce.17 = (f32[768]{0:T(1024)S(1)}, f32[768]{0:T(1024)S(1)}, f32[768]{0:T(1024)S(1)}, f32[768]{0:T(1024)S(1)}, f32[768]{0:T(1024)S(1)}, /*index=5*/f32[768]{0:T(1024)S(1)}, f32[768]{0:T(1024)S(1)}) all-reduce(f32[768]{0:T(1024)S(1)} %get-tuple-element.64, ...), channel_id=2, replica_groups=mesh['dp'=4,'expert'=8] {'dp','expert'}, use_global_device_ids=true, to_apply=%region_18.19.clone | all-reduce | flops 5376 | bytes 43008
  339.3 2.9 bitcast_convert_fusion.1
  342.2 2.9 bitcast_convert_fusion
  345.0 61.9 %reduce-scatter.7.cloned.1.call-done = f32[24,768]{1,0:T(8,128)} async-done(((f32[768,768]{1,0:T(8,128)}), f32[24,768]{1,0:T(8,128)}) %reduce-scatter.7.cloned.1.call-update) | async-done | bytes 73744 | tf_op jit(solution)/shard_map/reduce_scatter | solution.py:242
  406.9 124.8 %reduce-scatter.5.cloned.1.call-done = f32[24,2304]{1,0:T(8,128)} async-done(((f32[768,2304]{1,0:T(8,128)}), f32[24,2304]{1,0:T(8,128)}) %reduce-scatter.5.cloned.1.call-update) | async-done | bytes 221200 | tf_op jit(solution)/shard_map/reduce_scatter | solution.py:239
  (198 shorter events, 37.2 us)
Async XLA Ops:
  7.2 68.2 %all-gather.3.cloned.1.call-start = ((), (), s32[]{:S(2)}) async-start(), calls=%async_computation.8 | async-start | bytes 3649536 | tf_op jit(solution)/shard_map/all_gather | solution.py:73
  11.3 2.3 copy-start.36
  13.8 10.9 %copy-start.39 = (bf16[24]{0:T(256)(128)(2,1)S(1)}, bf16[24]{0:T(256)(128)(2,1)}, u32[]{:S(2)}) copy-start(bf16[24]{0:T(256)(128)(2,1)} %param.19) | copy-start | bytes 148
  13.8 11.1 %copy-start.40 = (bf16[24]{0:T(256)(128)(2,1)S(1)}, bf16[24]{0:T(256)(128)(2,1)}, u32[]{:S(2)}) copy-start(bf16[24]{0:T(256)(128)(2,1)} %param.18) | copy-start | bytes 148
  13.9 11.3 %copy-start.41 = (bf16[24]{0:T(256)(128)(2,1)S(1)}, bf16[24]{0:T(256)(128)(2,1)}, u32[]{:S(2)}) copy-start(bf16[24]{0:T(256)(128)(2,1)} %param.22) | copy-start | bytes 148
  13.9 11.5 %copy-start.42 = (bf16[24]{0:T(256)(128)(2,1)S(1)}, bf16[24]{0:T(256)(128)(2,1)}, u32[]{:S(2)}) copy-start(bf16[24]{0:T(256)(128)(2,1)} %param.21) | copy-start | bytes 148
  13.9 11.8 %copy-start.43 = (bf16[24]{0:T(256)(128)(2,1)S(1)}, bf16[24]{0:T(256)(128)(2,1)}, u32[]{:S(2)}) copy-start(bf16[24]{0:T(256)(128)(2,1)} %param.24) | copy-start | bytes 148
  13.9 12.0 %copy-start.44 = (bf16[24]{0:T(256)(128)(2,1)S(1)}, bf16[24]{0:T(256)(128)(2,1)}, u32[]{:S(2)}) copy-start(bf16[24]{0:T(256)(128)(2,1)} %param.26) | copy-start | bytes 148
  13.9 12.2 %copy-start.45 = (bf16[24]{0:T(256)(128)(2,1)S(1)}, bf16[24]{0:T(256)(128)(2,1)}, u32[]{:S(2)}) copy-start(bf16[24]{0:T(256)(128)(2,1)} %param.25) | copy-start | bytes 148
  13.9 54.4 %copy-start.6 = (bf16[1,197,768]{2,1,0:T(8,128)(2,1)S(1)}, bf16[1,197,768]{2,1,0:T(8,128)(2,1)}, u32[]{:S(2)}) copy-start(bf16[1,197,768]{2,1,0:T(8,128)(2,1)} %param.17) | copy-start | bytes 907780
  14.2 124.4 %copy-start.37 = (s32[394,1]{0,1:T(1,128)}, s32[394,1]{0,1:T(1,128)S(1)}, u32[]{:S(2)}) copy-start(s32[394,1]{0,1:T(1,128)S(1)} %compare_select_fusion) | copy-start | bytes 4732
  17.6 124.9 %all-to-all-start.2 = ((bf16[8,50,768]{2,1,0:T(8,128)(2,1)}), bf16[8,50,768]{2,1,0:T(8,128)(2,1)}, u32[]{:S(2)}, u32[]{:S(2)}) async-start(bf16[8,50,768]{2,1,0:T(8,128)(2,1)} %reshape.261), calls=%async_computation.2 | async-start | bytes 1376256 | tf_op jit(solution)/shard_map/all_to_all | solution.py:162
  23.9 107.5 %all-gather.5.cloned.1.call-start = ((), (), s32[]{:S(2)}) async-start(), calls=%async_computation.9 | async-start | bytes 1216512 | tf_op jit(solution)/shard_map/all_gather | solution.py:76
  68.8 6.6 %copy-start.34 = (f32[197]{0:T(256)}, f32[197]{0:T(256)S(1)}, u32[]{:S(2)}) copy-start(f32[197]{0:T(256)S(1)} %add_rsqrt_fusion.1) | copy-start | bytes 2368
  69.0 6.4 %copy-start.16 = (bf16[197,768]{1,0:T(8,128)(2,1)}, bf16[197,768]{1,0:T(8,128)(2,1)S(1)}, u32[]{:S(2)}) copy-start(bf16[197,768]{1,0:T(8,128)(2,1)S(1)} %fusion.54) | copy-start | bytes 907780
  69.1 64.4 %copy-start.21 = (f32[768]{0:T(1024)}, f32[768]{0:T(1024)S(1)}, u32[]{:S(2)}) copy-start(f32[768]{0:T(1024)S(1)} %convert_element_type.146) | copy-start | bytes 9220
  82.7 1.0 copy-start.5
  85.1 50.9 %copy-start.12 = (bf16[12,64,197]{2,1,0:T(8,128)(2,1)}, bf16[12,64,197]{2,1,0:T(8,128)(2,1)S(1)}, u32[]{:S(2)}) copy-start(bf16[12,64,197]{2,1,0:T(8,128)(2,1)S(1)} %convolution_convert_fusion.2) | copy-start | bytes 907780
  136.0 10.7 %copy-start.33 = (bf16[1,3072]{1,0:T(2,128)(2,1)S(1)}, bf16[1,3072]{1,0:T(2,128)(2,1)}, u32[]{:S(2)}) copy-start(bf16[1,3072]{1,0:T(2,128)(2,1)} %param.28) | copy-start | bytes 18436
  142.5 22.3 %all-to-all-start = ((bf16[8,50,768]{2,1,0:T(8,128)(2,1)}), bf16[8,50,768]{2,1,0:T(8,128)(2,1)S(1)}, u32[]{:S(2)}, u32[]{:S(2)}) async-start(bf16[8,50,768]{2,1,0:T(8,128)(2,1)} %reshape.255), calls=%async_computation | async-start | bytes 1376256 | tf_op jit(solution)/shard_map/all_to_all | solution.py:132
  146.1 193.2 %reduce-scatter.9.cloned.1.call-start = ((), (), s32[]{:S(2)}) async-start(), calls=%async_computation.12 | async-start | bytes 5898240 | tf_op jit(solution)/shard_map/reduce_scatter | solution.py:184
  165.8 7.2 %copy-start.19 = (bf16[400,768]{1,0:T(8,128)(2,1)S(1)}, bf16[400,768]{1,0:T(8,128)(2,1)}, u32[]{:S(2)}) copy-start(bf16[400,768]{1,0:T(8,128)(2,1)} %reshape.262) | copy-start | bytes 1843204
  173.1 9.0 %copy-start.20 = (bf16[400,768]{1,0:T(8,128)(2,1)S(1)}, bf16[400,768]{1,0:T(8,128)(2,1)}, u32[]{:S(2)}) copy-start(bf16[400,768]{1,0:T(8,128)(2,1)} %reshape.256) | copy-start | bytes 1843204
  180.6 1.5 copy-start.15
  186.4 155.7 %reduce-scatter.11.cloned.1.call-start = ((), (), s32[]{:S(2)}) async-start(), calls=%async_computation.13 | async-start | bytes 5898240 | tf_op jit(solution)/shard_map/reduce_scatter | solution.py:187
  198.2 4.8 copy-start.38
  199.2 22.5 %all-to-all-start.3 = ((bf16[8,50,768]{2,1,0:T(8,128)(2,1)}), bf16[8,50,768]{2,1,0:T(8,128)(2,1)S(1)}, u32[]{:S(2)}, u32[]{:S(2)}) async-start(bf16[8,50,768]{2,1,0:T(8,128)(2,1)} %reshape.263), calls=%async_computation.3 | async-start | bytes 1376256 | tf_op jit(solution)/shard_map/all_to_all | solution.py:172
  221.7 5.1 copy-start.14
  221.7 23.1 %all-to-all-start.1 = ((bf16[8,50,768]{2,1,0:T(8,128)(2,1)}), bf16[8,50,768]{2,1,0:T(8,128)(2,1)}, u32[]{:S(2)}, u32[]{:S(2)}) async-start(bf16[8,50,768]{2,1,0:T(8,128)(2,1)} %reshape.257), calls=%async_computation.1 | async-start | bytes 1376256 | tf_op jit(solution)/shard_map/all_to_all | solution.py:149
  225.9 181.0 %reduce-scatter.7.cloned.1.call-start = ((), (), s32[]{:S(2)}) async-start(), calls=%async_computation.11 | async-start | bytes 2433024 | tf_op jit(solution)/shard_map/reduce_scatter | solution.py:242
  232.1 13.9 %copy-start.27 = (s32[1024]{0:T(1024)S(1)}, s32[1024]{0:T(1024)}, u32[]{:S(2)}) copy-start(s32[1024]{0:T(1024)} %pad_clamp_fusion) | copy-start | bytes 12292
  246.0 5.5 %copy-start.22 = (f32[768]{0:T(1024)S(1)}, f32[768]{0:T(1024)}, u32[]{:S(2)}) copy-start(f32[768]{0:T(1024)} %copy-done.21) | copy-start | bytes 9220
  246.1 5.5 %copy-start.26 = (f32[197]{0:T(256)S(1)}, f32[197]{0:T(256)}, u32[]{:S(2)}) copy-start(f32[197]{0:T(256)} %copy-done.25) | copy-start | bytes 2368
  246.1 5.5 %copy-start.31 = (f32[197]{0:T(256)S(1)}, f32[197]{0:T(256)}, u32[]{:S(2)}) copy-start(f32[197]{0:T(256)} %copy-done.30) | copy-start | bytes 2368
  248.7 8.0 %copy-start.1 = (f32[197,768]{1,0:T(8,128)S(1)}, f32[197,768]{1,0:T(8,128)}, u32[]{:S(2)}) copy-start(f32[197,768]{1,0:T(8,128)} %copy-done) | copy-start | bytes 1815556
  251.6 5.1 copy-start.7
  251.6 5.1 copy-start.18
  256.7 1.9 copy-start.13
  260.5 271.2 %reduce-scatter.5.cloned.1.call-start = ((), (), s32[]{:S(2)}) async-start(), calls=%async_computation.10 | async-start | bytes 7299072 | tf_op jit(solution)/shard_map/reduce_scatter | solution.py:239
  265.9 2.0 copy-start.3
  266.0 2.2 copy-start.4
  269.2 1.2 copy-start.17
  274.5 17.2 %copy-start.24 = (f32[768]{0:T(1024)S(1)}, f32[768]{0:T(1024)}, u32[]{:S(2)}) copy-start(f32[768]{0:T(1024)} %copy-done.23) | copy-start | bytes 9220
  274.5 17.2 %copy-start.29 = (f32[197]{0:T(256)S(1)}, f32[197]{0:T(256)}, u32[]{:S(2)}) copy-start(f32[197]{0:T(256)} %copy-done.28) | copy-start | bytes 2368
  274.5 17.2 %copy-start.35 = (f32[197]{0:T(256)S(1)}, f32[197]{0:T(256)}, u32[]{:S(2)}) copy-start(f32[197]{0:T(256)} %copy-done.34) | copy-start | bytes 2368
  291.7 4.0 copy-start.10
  295.7 1.8 copy-start.8
  295.8 2.1 copy-start.32
  (9 other events, 7.0 us)
Sparse Core Ops, SparseCore 0:
  11.0 64.3 all-gather.2
  78.4 52.9 all-gather.4
  186.6 54.9 reduce-scatter.8
  244.4 57.1 reduce-scatter.10
  307.3 99.6 reduce-scatter.6
  413.1 118.6 reduce-scatter.4
where the time goes:
time: 545 us; the launch traced here: 539 us
  waiting for transfers between devices  273 us (50%)
  blocking collectives  89.3 us (16%)
  matrix products  61.4 us (11%)
  local copies, waits for them, and re-layouts  51.2 us (9%)
  other arithmetic  28.2 us (5%)
  starting transfers between devices  18.8 us (3%)
  between operations  16.5 us (3%)
    reduce_scatter x1, waiting for transfers between devices, per_device(): lax.psum_scatter(qkv_weight_grad, ('dp', 'expert'), scatter_dimension=0,...  125 us
    unnamed x3, blocking collectives  89.3 us
    reduce_scatter x1, waiting for transfers between devices, per_device(): lax.psum_scatter(out_weight_grad, ('dp', 'expert'), scatter_dimension=0,...  61.9 us
    all_gather x1, waiting for transfers between devices, per_device(): lax.all_gather(out_weight, ('dp', 'expert'), axis=0, tiled=True)  46.3 us
    unnamed x119, local copies, waits for them, and re-layouts  16.2 us
    all_to_all x1, waiting for transfers between devices, per_device(): lax.all_to_all(outgoing.reshape(expert_count, capacity, D), 'expert', spl...  16.1 us
  transfers between devices with their start and end apart: 10, of which 7 were waited for; matrix products, arithmetic and copies ran while one was open for 21% of the time, Pallas kernels for 0%

commit v1 on v0

--- a/solution.py
+++ b/solution.py
@@ -8,6 +8,28 @@
 HEAD_DIM = 64
 SEQ = 197
 EPSILON = 1e-06
+
+
+def in_order(parts, dim):
+    dims = list(parts.shape[1:])
+    dims[dim] *= parts.shape[0]
+    return jnp.moveaxis(parts, 0, dim).reshape(dims)
+
+
+def collected_by_bits(array, axis):
+    size = lax.axis_size(axis)
+    pieces = array[None]
+    for level in range(size.bit_length() - 1):
+        bit = 1 << level
+        other = lax.ppermute(pieces, axis, [(i, i ^ bit) for i in range(size)])
+        both = jnp.stack([pieces, other])
+        upper = lax.axis_index(axis) >> level & 1
+        pieces = jnp.where(upper == 0, both, both[::-1]).reshape(-1, *array.shape)
+    return pieces
+
+
+def collect(array, axis, dim):
+    return in_order(collected_by_bits(array, axis), dim)
 
 
 def to_half(values):
@@ -73,7 +95,7 @@
         lax.all_gather(qkv_weight, ("dp", "expert"), axis=0, tiled=True),
         lax.all_gather(q_bias, ("dp", "expert"), axis=0, tiled=True),
         lax.all_gather(v_bias, ("dp", "expert"), axis=0, tiled=True),
-        lax.all_gather(out_weight, ("dp", "expert"), axis=0, tiled=True),
+        collect(out_weight, ("dp", "expert"), 0),
         lax.all_gather(out_bias, ("dp", "expert"), axis=0, tiled=True),
         lax.all_gather(ln2_gain, ("dp", "expert"), axis=0, tiled=True),
         lax.all_gather(ln2_bias, ("dp", "expert"), axis=0, tiled=True),

time: 545 us -> 518 us (0.950)
  waiting for transfers between devices: 273 us -> 235 us
  starting transfers between devices: 18.8 us -> 26.8 us
  blocking collectives: 89.3 us -> 95.7 us
    all_gather x1 -> x0, waiting for transfers between devices: 46.3 us -> none  [per_device(): lax.all_gather(out_weight, ('dp', 'expert'), axis=0, tiled=True)]
    ppermute x0 -> x5, waiting for transfers between devices: none -> 10.7 us  [collected_by_bits(): other = lax.ppermute(pieces, axis, [(i, i ^ bit) for i in range(size)])]
    ppermute x0 -> x5, starting transfers between devices: none -> 9.03 us  [collected_by_bits(): other = lax.ppermute(pieces, axis, [(i, i ^ bit) for i in range(size)])]
    unnamed x3, blocking collectives: 89.3 us -> 95.7 us
    all_gather x1, waiting for transfers between devices: 6.28 us -> 0.01 us  [per_device(): lax.all_gather(qkv_weight, ('dp', 'expert'), axis=0, tiled=True)]
    unnamed x119 -> x91, local copies, waits for them, and re-layouts: 16.2 us -> 14.5 us
  transfers between devices with their start and end apart: 10 -> 14, of which waited for: 7 -> 8; matrix products, arithmetic and copies ran while one was open for 21% -> 22% of each run, Pallas kernels for 0% -> 0%
where the time goes in v1:
time: 518 us; the launch traced here: 510 us
  waiting for transfers between devices  235 us (45%)
  blocking collectives  95.7 us (18%)
  matrix products  60.7 us (12%)
  local copies, waits for them, and re-layouts  48.8 us (9%)
  other arithmetic  27.4 us (5%)
  starting transfers between devices  26.8 us (5%)
  between operations  16.4 us (3%)
    reduce_scatter x1, waiting for transfers between devices, per_device(): lax.psum_scatter(qkv_weight_grad, ('dp', 'expert'), scatter_dimension=0,...  125 us
    unnamed x3, blocking collectives  95.7 us
    reduce_scatter x1, waiting for transfers between devices, per_device(): lax.psum_scatter(out_weight_grad, ('dp', 'expert'), scatter_dimension=0,...  60.6 us
    all_to_all x1, waiting for transfers between devices, per_device(): lax.all_to_all(outgoing.reshape(expert_count, capacity, D), 'expert', spl...  17.3 us
    unnamed x91, local copies, waits for them, and re-layouts  14.5 us
    all_to_all x1, waiting for transfers between devices, per_device(): lax.all_to_all(grad_rows.reshape(expert_count, capacity, D), 'expert', sp...  12.3 us
    ppermute x5, waiting for transfers between devices, collected_by_bits(): other = lax.ppermute(pieces, axis, [(i, i ^ bit) for i in range(size)])  10.7 us
  transfers between devices with their start and end apart: 14, of which 8 were waited for; matrix products, arithmetic and copies ran while one was open for 22% of the time, Pallas kernels for 0%

profile of v1, /device:TPU:0, one launch (start us, length us, event | category | flops | bytes accessed | tf_op | source)
XLA Modules:
  0.0 510.5 jit_solution(13605521798339018455)
XLA Ops:
  14.0 2.6 collective-permute-start.1
  16.7 2.9 collective-permute-done.1
  19.7 2.8 collective-permute-start.2
  22.5 2.3 scatter_custom_fusion.1
  25.9 4.3 all-to-all-start.2
  32.4 7.3 %collective-permute-done.3 = bf16[8,24,768]{2,1,0:T(8,128)(2,1)S(1)} collective-permute-done((bf16[8,24,768]{2,1,0:T(8,128)(2,1)S(1)}, bf16[8,24,768]{2,1,0:T(8,128)(2,1)S(1)}, u32[]{:S(2)}, u32[]{:S(2)}) %collective-permute-start.3) | collective-permute-done | bytes 294944 | tf_op jit(solution)/shard_map/ppermute | solution.py:24
  39.9 1.6 collective-permute-start.4
  43.4 47.9 %all-reduce.18 = (bf16[768]{0:T(1024)(128)(2,1)S(1)}, bf16[768]{0:T(1024)(128)(2,1)S(1)}, bf16[768]{0:T(1024)(128)(2,1)S(1)}, bf16[768]{0:T(1024)(128)(2,1)S(1)}...) all-reduce(bf16[768]{0:T(1024)(128)(2,1)S(1)} %dynamic-update-slice, ...), channel_id=1, replica_groups=mesh['dp'=4,'expert'=8] {'dp','expert'}, use_global_device_ids=true, to_apply=%add.2 | all-reduce | flops 5376 | bytes 21504
  93.0 2.9 fusion.17
  98.0 2.1 fusion.20
  100.3 1.9 convolution_convert_fusion.2
  104.9 2.7 reshape.315
  107.5 2.9 scatter_custom_fusion
  111.4 4.2 all-to-all-start
  117.1 17.3 %all-to-all-done = bf16[8,50,768]{2,1,0:T(8,128)(2,1)} async-done(((bf16[8,50,768]{2,1,0:T(8,128)(2,1)}), bf16[8,50,768]{2,1,0:T(8,128)(2,1)}, u32[]{:S(2)}, u32[]{:S(2)}) %all-to-all-start) | async-done | bytes 614432 | tf_op jit(solution)/shard_map/all_to_all | solution.py:154
  134.5 2.1 reshape.272
  136.5 7.2 %multiply_convert_fusion = (bf16[400,3072]{1,0:T(8,128)(2,1)}, f32[400,3072]{1,0:T(8,128)S(1)}) fusion(f32[3072]{0:T(1024)S(1)} %bitcast.208, bf16[400,768]{1,0:T(8,128)(2,1)} %reshape.272, bf16[1,768,3072]{2,1,0:T(8,128)(2,1)} %param.27), kind=kOutput, calls=%fused_computation.17 | convolution fusion | flops 1899724800 | bytes 12718080 | tf_op jit(solution)/shard_map/dot_general | solution.py:163
  143.7 7.4 %fusion.8 = bf16[400,3072]{1,0:T(8,128)(2,1)S(1)} fusion(f32[400,3072]{1,0:T(8,128)S(1)} %get-tuple-element.93, bf16[400,768]{1,0:T(8,128)(2,1)S(1)} %reshape.278, bf16[1,3072,768]{2,1,0:T(8,128)(2,1)} %param.29, f32[3072]{0:T(1024)S(1)} %bitcast.209), kind=kOutput, calls=%fused_computation.16 | convolution fusion | flops 1913241600 | bytes 12718080 | tf_op jit(solution)/shard_map/dot_general | solution.py:191
  151.2 1.5 copy-done.15
  152.7 4.4 convolution_convert_fusion.1
  157.1 6.7 %convolution_convert_fusion = bf16[3072,768]{1,0:T(8,128)(2,1)} fusion(bf16[400,3072]{1,0:T(8,128)(2,1)} %get-tuple-element.92, bf16[400,768]{1,0:T(8,128)(2,1)S(1)} %reshape.278), kind=kOutput, calls=%fused_computation.8 | convolution fusion | flops 1889796096 | bytes 7790592 | tf_op jit(solution)/shard_map/dot_general | solution.py:202
  163.8 5.2 %fusion.37 = bf16[400,768]{1,0:T(8,128)(2,1)S(1)} fusion(bf16[400,3072]{1,0:T(8,128)(2,1)} %copy-done.15, bf16[1,768,3072]{2,1,0:T(8,128)(2,1)} %param.27), kind=kOutput, calls=%fused_computation.41 | convolution fusion | flops 1887744000 | bytes 7790592 | tf_op jit(solution)/shard_map/dot_general | solution.py:193
  170.1 4.4 all-to-all-start.3
  174.5 5.5 %fusion.34 = bf16[400,768]{1,0:T(8,128)(2,1)S(1)} fusion(bf16[400,3072]{1,0:T(8,128)(2,1)} %get-tuple-element.92, bf16[1,3072,768]{2,1,0:T(8,128)(2,1)} %param.29, f32[768]{0:T(1024)S(1)} %convert_reduce_fusion.2), kind=kOutput, calls=%fused_computation.40 | convolution fusion | flops 1888051200 | bytes 7793664 | tf_op jit(solution)/shard_map/dot_general | solution.py:168
  181.0 12.3 %all-to-all-done.3 = bf16[8,50,768]{2,1,0:T(8,128)(2,1)} async-done(((bf16[8,50,768]{2,1,0:T(8,128)(2,1)}), bf16[8,50,768]{2,1,0:T(8,128)(2,1)}, u32[]{:S(2)}, u32[]{:S(2)}) %all-to-all-start.3) | async-done | bytes 614432 | tf_op jit(solution)/shard_map/all_to_all | solution.py:194
  193.3 4.2 all-to-all-start.1
  199.0 2.7 gather_fusion.1
  201.7 2.8 reshape.290
  204.4 3.6 reduce_sum.214
  208.0 8.4 %all-to-all-done.1 = bf16[8,50,768]{2,1,0:T(8,128)(2,1)} async-done(((bf16[8,50,768]{2,1,0:T(8,128)(2,1)}), bf16[8,50,768]{2,1,0:T(8,128)(2,1)}, u32[]{:S(2)}, u32[]{:S(2)}) %all-to-all-start.1) | async-done | bytes 614432 | tf_op jit(solution)/shard_map/all_to_all | solution.py:171
  217.7 2.7 gather_fusion
  220.3 2.8 reshape.288
  223.1 1.7 multiply_reduce_fusion.2
  224.9 2.8 multiply_reduce_fusion.1
  229.6 1.9 fusion.79
  231.8 2.5 convolution_convert_fusion.3
  235.5 3.1 fusion.28
  238.6 2.1 convolution_bitcast_fusion
  243.1 4.1 fusion.78
  251.0 2.2 reduce_sum.227
  253.2 10.5 %all-reduce.19 = (bf16[3072]{0:T(1024)(128)(2,1)S(1)}, bf16[768]{0:T(1024)(128)(2,1)S(1)}) all-reduce(bf16[3072]{0:T(1024)(128)(2,1)S(1)} %reduce_sum.227, bf16[768]{0:T(1024)(128)(2,1)S(1)} %reduce_sum.228), channel_id=12, replica_groups=mesh['dp'=4,'expert'=8] {'dp'}, use_global_device_ids=true, to_apply=%region_35.36.clone | all-reduce | flops 3840 | bytes 15360
  265.0 3.9 fusion.60
  269.3 1.4 copy.64
  271.1 37.3 %all-reduce.17 = (f32[768]{0:T(1024)S(1)}, f32[768]{0:T(1024)S(1)}, f32[768]{0:T(1024)S(1)}, f32[768]{0:T(1024)S(1)}, f32[768]{0:T(1024)S(1)}, /*index=5*/f32[768]{0:T(1024)S(1)}, f32[768]{0:T(1024)S(1)}) all-reduce(f32[768]{0:T(1024)S(1)} %get-tuple-element.64, ...), channel_id=2, replica_groups=mesh['dp'=4,'expert'=8] {'dp','expert'}, use_global_device_ids=true, to_apply=%region_18.19.clone | all-reduce | flops 5376 | bytes 43008
  312.5 2.9 bitcast_convert_fusion.1
  315.4 2.9 bitcast_convert_fusion
  318.3 60.6 %reduce-scatter.7.cloned.1.call-done = f32[24,768]{1,0:T(8,128)} async-done(((f32[768,768]{1,0:T(8,128)}), f32[24,768]{1,0:T(8,128)}) %reduce-scatter.7.cloned.1.call-update) | async-done | bytes 73744 | tf_op jit(solution)/shard_map/reduce_scatter | solution.py:264
  378.8 124.7 %reduce-scatter.5.cloned.1.call-done = f32[24,2304]{1,0:T(8,128)} async-done(((f32[768,2304]{1,0:T(8,128)}), f32[24,2304]{1,0:T(8,128)}) %reduce-scatter.5.cloned.1.call-update) | async-done | bytes 221200 | tf_op jit(solution)/shard_map/reduce_scatter | solution.py:261
  (187 shorter events, 40.1 us)
Async XLA Ops:
  7.2 85.8 %all-gather.2.cloned.1.call-start = ((), (), s32[]{:S(2)}) async-start(), calls=%async_computation.8 | async-start | bytes 3649536 | tf_op jit(solution)/shard_map/all_gather | solution.py:95
  7.9 6.1 %collective-permute-start = (bf16[1,24,768]{2,1,0:T(8,128)(2,1)}, bf16[1,24,768]{2,1,0:T(8,128)(2,1)S(1)}, u32[]{:S(2)}, u32[]{:S(2)}) collective-permute-start(bf16[1,24,768]{2,1,0:T(8,128)(2,1)} %bitcast.205), channel_id=1, source_target_pairs={{0,1},{1,0},{2,3},{3,2},{4,5},{5,4},{6,7},{7,6},{8,9},{9,8},{10,11... | collective-permute-start | bytes 110600 | tf_op jit(solution)/shard_map/ppermute | solution.py:24
  10.8 2.3 copy-start.22
  12.3 1.4 copy-start.23
  12.3 1.7 copy-start.20
  14.0 5.6 %collective-permute-start.1 = (bf16[2,24,768]{2,1,0:T(8,128)(2,1)S(1)}, bf16[2,24,768]{2,1,0:T(8,128)(2,1)S(1)}, u32[]{:S(2)}, u32[]{:S(2)}) collective-permute-start(bf16[2,24,768]{2,1,0:T(8,128)(2,1)S(1)} %get-tuple-element.89), channel_id=1, source_target_pairs={{0,2},{1,3},{2,0},{3,1},{4,6},{5,7},{6,4},{7,5},{8,10},{9,11},{10,... | collective-permute-start | bytes 221192 | tf_op jit(solution)/shard_map/ppermute | solution.py:24
  19.6 12.7 %copy-start.7 = (bf16[1,197,768]{2,1,0:T(8,128)(2,1)S(1)}, bf16[1,197,768]{2,1,0:T(8,128)(2,1)}, u32[]{:S(2)}) copy-start(bf16[1,197,768]{2,1,0:T(8,128)(2,1)} %param.17) | copy-start | bytes 907780
  19.7 11.1 %collective-permute-start.2 = (bf16[4,24,768]{2,1,0:T(8,128)(2,1)S(1)}, bf16[4,24,768]{2,1,0:T(8,128)(2,1)S(1)}, u32[]{:S(2)}, u32[]{:S(2)}) collective-permute-start(bf16[4,24,768]{2,1,0:T(8,128)(2,1)S(1)} %bitcast.199), channel_id=1, source_target_pairs={{0,4},{1,5},{2,6},{3,7},{4,0},{5,1},{6,2},{7,3},{8,12},{9,13},{10,... | collective-permute-start | bytes 442376 | tf_op jit(solution)/shard_map/ppermute | solution.py:24
  25.9 15.9 %copy-start.25 = (bf16[24]{0:T(256)(128)(2,1)S(1)}, bf16[24]{0:T(256)(128)(2,1)}, u32[]{:S(2)}) copy-start(bf16[24]{0:T(256)(128)(2,1)} %param.19) | copy-start | bytes 148
  25.9 16.1 %copy-start.26 = (bf16[24]{0:T(256)(128)(2,1)S(1)}, bf16[24]{0:T(256)(128)(2,1)}, u32[]{:S(2)}) copy-start(bf16[24]{0:T(256)(128)(2,1)} %param.18) | copy-start | bytes 148
  25.9 16.3 %copy-start.27 = (bf16[24]{0:T(256)(128)(2,1)S(1)}, bf16[24]{0:T(256)(128)(2,1)}, u32[]{:S(2)}) copy-start(bf16[24]{0:T(256)(128)(2,1)} %param.22) | copy-start | bytes 148
  25.9 16.6 %copy-start.28 = (bf16[24]{0:T(256)(128)(2,1)S(1)}, bf16[24]{0:T(256)(128)(2,1)}, u32[]{:S(2)}) copy-start(bf16[24]{0:T(256)(128)(2,1)} %param.21) | copy-start | bytes 148
  25.9 16.8 %copy-start.29 = (bf16[24]{0:T(256)(128)(2,1)S(1)}, bf16[24]{0:T(256)(128)(2,1)}, u32[]{:S(2)}) copy-start(bf16[24]{0:T(256)(128)(2,1)} %param.24) | copy-start | bytes 148
  25.9 17.0 %copy-start.30 = (bf16[24]{0:T(256)(128)(2,1)S(1)}, bf16[24]{0:T(256)(128)(2,1)}, u32[]{:S(2)}) copy-start(bf16[24]{0:T(256)(128)(2,1)} %param.26) | copy-start | bytes 148
  25.9 17.2 %copy-start.31 = (bf16[24]{0:T(256)(128)(2,1)S(1)}, bf16[24]{0:T(256)(128)(2,1)}, u32[]{:S(2)}) copy-start(bf16[24]{0:T(256)(128)(2,1)} %param.25) | copy-start | bytes 148
  25.9 85.5 %all-to-all-start.2 = ((bf16[8,50,768]{2,1,0:T(8,128)(2,1)}), bf16[8,50,768]{2,1,0:T(8,128)(2,1)}, u32[]{:S(2)}, u32[]{:S(2)}) async-start(bf16[8,50,768]{2,1,0:T(8,128)(2,1)} %reshape.277), calls=%async_computation.2 | async-start | bytes 1376256 | tf_op jit(solution)/shard_map/all_to_all | solution.py:184
  30.9 8.9 %collective-permute-start.3 = (bf16[8,24,768]{2,1,0:T(8,128)(2,1)S(1)}, bf16[8,24,768]{2,1,0:T(8,128)(2,1)S(1)}, u32[]{:S(2)}, u32[]{:S(2)}) collective-permute-start(bf16[8,24,768]{2,1,0:T(8,128)(2,1)S(1)} %bitcast.197), channel_id=1, source_target_pairs={{0,8},{1,9},{2,10},{3,11},{4,12},{5,13},{6,14},{7,15},{8,0},{9,1},... | collective-permute-start | bytes 884744 | tf_op jit(solution)/shard_map/ppermute | solution.py:24
  39.9 51.7 %collective-permute-start.4 = (bf16[16,24,768]{2,1,0:T(8,128)(2,1)S(1)}, bf16[16,24,768]{2,1,0:T(8,128)(2,1)S(1)}, u32[]{:S(2)}, u32[]{:S(2)}) collective-permute-start(bf16[16,24,768]{2,1,0:T(8,128)(2,1)S(1)} %bitcast.195), channel_id=1, source_target_pairs={{0,16},{1,17},{2,18},{3,19},{4,20},{5,21},{6,22},{7,23},{8,24},{9,... | collective-permute-start | bytes 1769480 | tf_op jit(solution)/shard_map/ppermute | solution.py:24
  91.5 1.5 copy-start.16
  96.5 1.0 copy-start.2
  100.1 2.0 copy-start.6
  100.3 2.7 copy-start.5
  102.1 2.7 copy-start.13
  102.7 0.8 copy-start
  104.9 11.0 %copy-start.21 = (bf16[1,3072]{1,0:T(2,128)(2,1)S(1)}, bf16[1,3072]{1,0:T(2,128)(2,1)}, u32[]{:S(2)}) copy-start(bf16[1,3072]{1,0:T(2,128)(2,1)} %param.28) | copy-start | bytes 18436
  111.4 23.0 %all-to-all-start = ((bf16[8,50,768]{2,1,0:T(8,128)(2,1)}), bf16[8,50,768]{2,1,0:T(8,128)(2,1)}, u32[]{:S(2)}, u32[]{:S(2)}) async-start(bf16[8,50,768]{2,1,0:T(8,128)(2,1)} %reshape.271), calls=%async_computation | async-start | bytes 1376256 | tf_op jit(solution)/shard_map/all_to_all | solution.py:154
  115.6 196.9 %reduce-scatter.9.cloned.1.call-start = ((), (), s32[]{:S(2)}) async-start(), calls=%async_computation.11 | async-start | bytes 5898240 | tf_op jit(solution)/shard_map/reduce_scatter | solution.py:206
  143.7 8.9 %copy-start.19 = (bf16[400,768]{1,0:T(8,128)(2,1)S(1)}, bf16[400,768]{1,0:T(8,128)(2,1)}, u32[]{:S(2)}) copy-start(bf16[400,768]{1,0:T(8,128)(2,1)} %reshape.272) | copy-start | bytes 1843204
  151.2 1.5 copy-start.15
  157.1 158.3 %reduce-scatter.11.cloned.1.call-start = ((), (), s32[]{:S(2)}) async-start(), calls=%async_computation.12 | async-start | bytes 5898240 | tf_op jit(solution)/shard_map/reduce_scatter | solution.py:209
  169.0 5.5 %copy-start.24 = (bf16[1,768]{1,0:T(2,128)(2,1)S(1)}, bf16[1,768]{1,0:T(2,128)(2,1)}, u32[]{:S(2)}) copy-start(bf16[1,768]{1,0:T(2,128)(2,1)} %param.30) | copy-start | bytes 4612
  170.1 23.3 %all-to-all-start.3 = ((bf16[8,50,768]{2,1,0:T(8,128)(2,1)}), bf16[8,50,768]{2,1,0:T(8,128)(2,1)}, u32[]{:S(2)}, u32[]{:S(2)}) async-start(bf16[8,50,768]{2,1,0:T(8,128)(2,1)} %reshape.279), calls=%async_computation.3 | async-start | bytes 1376256 | tf_op jit(solution)/shard_map/all_to_all | solution.py:194
  193.3 23.1 %all-to-all-start.1 = ((bf16[8,50,768]{2,1,0:T(8,128)(2,1)}), bf16[8,50,768]{2,1,0:T(8,128)(2,1)}, u32[]{:S(2)}, u32[]{:S(2)}) async-start(bf16[8,50,768]{2,1,0:T(8,128)(2,1)} %reshape.273), calls=%async_computation.1 | async-start | bytes 1376256 | tf_op jit(solution)/shard_map/all_to_all | solution.py:171
  197.5 181.3 %reduce-scatter.7.cloned.1.call-start = ((), (), s32[]{:S(2)}) async-start(), calls=%async_computation.10 | async-start | bytes 2433024 | tf_op jit(solution)/shard_map/reduce_scatter | solution.py:264
  220.3 7.4 %copy-start.1 = (f32[197,768]{1,0:T(8,128)S(1)}, f32[197,768]{1,0:T(8,128)}, u32[]{:S(2)}) copy-start(f32[197,768]{1,0:T(8,128)} %copy-done) | copy-start | bytes 1815556
  223.1 4.6 copy-start.8
  223.1 4.6 copy-start.18
  227.7 1.9 copy-start.14
  228.8 0.8 copy-start.10
  231.5 272.0 %reduce-scatter.5.cloned.1.call-start = ((), (), s32[]{:S(2)}) async-start(), calls=%async_computation.9 | async-start | bytes 7299072 | tf_op jit(solution)/shard_map/reduce_scatter | solution.py:261
  238.6 2.1 copy-start.3
  238.6 2.3 copy-start.4
  241.9 1.2 copy-start.17
  242.1 1.0 copy-start.12
  247.2 0.7 copy-start.32
  265.0 4.0 copy-start.11
  269.0 1.8 copy-start.9
Sparse Core Ops, SparseCore 0:
  11.0 67.5 all-gather.1
  157.2 56.1 reduce-scatter.8
  216.4 57.3 reduce-scatter.10
  279.4 99.3 reduce-scatter.6
  384.9 118.5 reduce-scatter.4
